TPU v7x, 512 devices: a whole 4x4x16 slice. The times are simulated.
512 devices in a mesh: gx: 32 (over z, x_lo), gy: 16 (over x_hi, y, core).
Axes of the slice: x: 4 (x_hi: 2, x_lo: 2; x = x_hi * 2 + x_lo), y: 4, z: 16, core: 2. Of those that a mesh axis runs over, the one named last changes fastest.
Arguments:
- adjoint_forcing: float32 [4, 6, 1024, 4096], P(None, None, 'gx', 'gy'), may hold values from -6 to 6
- field_mixing: float32 [4, 4], replicated, may hold values from -3 to 3
- time_mixing: float32 [6, 6], replicated, may hold values from -2.5 to 2.5
- kernel_east: float32 [21], replicated, may hold values from 0.1 to 1
- kernel_north: float32 [21], replicated, may hold values from 0.1 to 1
- spatial_modes: bfloat16 [1024, 4096, 256], P('gx', 'gy'), may hold values from -0.00390625 to 0.00390625
- coefficients: float32 [256, 24], P('gy'), may hold values from -6 to 6
Outputs:
- gradient: float32 [256, 24], P('gy')
All inputs are finite; a program needn't handle non-finite values.
Results may differ from a plain program's by a relative error of at most 0.0029.
Values sent between devices are 32-bit elements; how exact they have to be, the bound alone decides.
A program may use at most 64 MiB of HBM per device.

v0:
```python
import jax
import jax.numpy as jnp
from jax import lax
from jax.sharding import PartitionSpec as P


def padded(block, sides, width):
    for axis, dim in sides:
        count = lax.axis_size(axis)
        forward = [(i, i + 1) for i in range(count - 1)]
        backward = [(target, source) for source, target in forward]
        low = lax.ppermute(
            lax.slice_in_dim(block, block.shape[dim] - width, None, axis=dim), axis, forward
        )
        high = lax.ppermute(lax.slice_in_dim(block, 0, width, axis=dim), axis, backward)
        block = jnp.concatenate([low, block, high], axis=dim)
    return block


def smooth_valid(extended, taps, axis, count):
    total = taps[0] * lax.slice_in_dim(extended, 0, count, axis=axis)
    for j in range(1, taps.shape[0]):
        total = total + taps[j] * lax.slice_in_dim(extended, j, j + count, axis=axis)
    return total


def local(
    adjoint_forcing,
    field_mixing,
    time_mixing,
    kernel_east,
    kernel_north,
    spatial_modes,
    coefficients,
):
    fields, levels, width_x, width_y = adjoint_forcing.shape
    reach = (kernel_east.shape[0] - 1) // 2
    mixed = jnp.einsum(
        "gf,st,gsxy->ftxy",
        field_mixing,
        time_mixing,
        adjoint_forcing,
        precision=lax.Precision.HIGHEST,
    )
    wide_x = padded(mixed, (("gx", 2),), reach)
    along_x = smooth_valid(wide_x, kernel_east, 2, width_x)
    wide_y = padded(along_x, (("gy", 3),), reach)
    smoothed = smooth_valid(wide_y, kernel_north, 3, width_y)
    smoothed = smoothed.astype(jnp.bfloat16)
    flat_state = smoothed.reshape(fields * levels, width_x * width_y)
    flat_modes = spatial_modes.reshape(width_x * width_y, spatial_modes.shape[2])
    projection = lax.dot_general(
        flat_modes, flat_state, (((0,), (1,)), ((), ())), preferred_element_type=jnp.float32
    )
    owned = coefficients.shape[0]
    total = lax.psum(projection, ("gx", "gy"))
    mine = lax.dynamic_slice_in_dim(total, lax.axis_index("gy") * owned, owned, 0)
    return coefficients + mine


def solution(mesh):
    in_specs = (P(None, None, "gx", "gy"), P(), P(), P(), P(), P("gx", "gy", None), P("gy", None))
    out_specs = P("gy", None)
    return jax.shard_map(local, mesh=mesh, in_specs=in_specs, out_specs=out_specs, check_vma=False)
```

profile of v0, /device:TPU:1, one launch (start us, length us, event | category | flops | bytes accessed | tf_op | source)
XLA Modules:
  0.0 193.7 jit_solution(18179628404483678090)
XLA Ops:
  0.0 0.0 copy-start
  0.0 3.1 %fusion.118 = f32[6,32,256,4]{2,3,1,0:T(4,128)S(1)} fusion(f32[4,6,32,256]{3,2,1,0:T(8,128)} %param.7, f32[4,4]{1,0:T(4,128)} %param.8), kind=kOutput, calls=%fused_computation.196 | convolution fusion | flops 9437184 | bytes 1572928 | tf_op jit(solution)/shard_map/gf,st,gsxy->ftxy/dot_general | solution.py:38
  3.1 0.0 copy-done
  3.1 0.0 copy-start.2
  3.1 0.0 copy-start.3
  3.1 1.5 convolution_bitcast_fusion
  4.6 0.1 fusion.123
  4.6 4.0 %collective-permute-start = (f32[4,6,10,256]{3,1,0,2:T(8,128)S(1)}, f32[4,6,10,256]{3,1,0,2:T(8,128)S(1)}, u32[]{:S(2)}, u32[]{:S(2)}) collective-permute-start(f32[4,6,10,256]{3,1,0,2:T(8,128)S(1)} %get-tuple-element.7), channel_id=1, source_target_pairs={{0,16},{16,32},{32,48},{48,64},{64,80},{80,96},{96,112},{112,128},... | collective-permute-start | bytes 737288 | tf_op jit(solution)/shard_map/ppermute | solution.py:12
  8.6 1.3 collective-permute-start.1
  9.9 0.0 copy-done.2
  9.9 0.7 fusion.127
  10.6 0.7 fusion.126
  11.3 0.0 copy-done.3
  11.3 0.7 fusion.124
  12.0 0.6 collective-permute-done
  12.6 4.0 %collective-permute-done.1 = f32[4,6,10,256]{3,1,0,2:T(8,128)S(1)} collective-permute-done((f32[4,6,10,256]{3,1,0,2:T(8,128)S(1)}, f32[4,6,10,256]{3,1,0,2:T(8,128)S(1)}, u32[]{:S(2)}, u32[]{:S(2)}) %collective-permute-start.1) | collective-permute-done | bytes 245792 | tf_op jit(solution)/shard_map/ppermute | solution.py:15
  16.5 15.8 %fusion.3 = f32[4,6,32,256]{3,1,0,2:T(8,128)S(1)} fusion(f32[4,6,32,256]{3,1,0,2:T(8,128)S(1)} %convolution_bitcast_fusion, f32[4,6,10,256]{3,1,0,2:T(8,128)S(1)} %collective-permute-done.1, f32[4,6,10,256]{3,1,0,2:T(8,128)S(1)} %collective-permute-done, f32[]{:T(128)} %bitcast.24, f32[]{:T(128)} %bitcast.23, f32[]{:T(128)} %bitcast.22, f32[]{:T(128)} %bitcast.21, ...), kind=kLoop, calls=%fused_computation.77 | loop fusion | flops 11993088 | bytes 2064468 | tf_op jit(solution)/shard_map/add | solution.py:23
  32.4 0.2 fusion.122
  32.6 10.0 %collective-permute-start.2 = (f32[4,6,32,10]{3,1,0,2:T(8,128)S(1)}, f32[4,6,32,10]{3,1,0,2:T(8,128)S(1)}, u32[]{:S(2)}, u32[]{:S(2)}) collective-permute-start(f32[4,6,32,10]{3,1,0,2:T(8,128)S(1)} %get-tuple-element.5), channel_id=1, source_target_pairs={{0,1},{1,2},{2,3},{3,4},{4,5},{5,6},{6,7},{7,8},{8,9},{9,10},{10,1... | collective-permute-start | bytes 92168 | tf_op jit(solution)/shard_map/ppermute | solution.py:12
  42.6 1.9 collective-permute-start.3
  44.6 0.7 fusion.125
  45.2 3.5 %collective-permute-done.2 = f32[4,6,32,10]{3,1,0,2:T(8,128)S(1)} collective-permute-done((f32[4,6,32,10]{3,1,0,2:T(8,128)S(1)}, f32[4,6,32,10]{3,1,0,2:T(8,128)S(1)}, u32[]{:S(2)}, u32[]{:S(2)}) %collective-permute-start.2) | collective-permute-done | bytes 30752 | tf_op jit(solution)/shard_map/ppermute | solution.py:12
  48.7 4.4 %collective-permute-done.3 = f32[4,6,32,10]{3,1,0,2:T(8,128)S(1)} collective-permute-done((f32[4,6,32,10]{3,1,0,2:T(8,128)S(1)}, f32[4,6,32,10]{3,1,0,2:T(8,128)S(1)}, u32[]{:S(2)}, u32[]{:S(2)}) %collective-permute-start.3) | collective-permute-done | bytes 30752 | tf_op jit(solution)/shard_map/ppermute | solution.py:15
  53.1 0.0 copy-start.1
  53.1 22.8 %fusion.60 = bf16[4,6,32,256]{3,1,0,2:T(8,128)(2,1)S(1)} fusion(f32[4,6,32,256]{3,1,0,2:T(8,128)S(1)} %fusion.3, f32[4,6,32,10]{3,1,0,2:T(8,128)S(1)} %collective-permute-done.3, f32[4,6,32,10]{3,1,0,2:T(8,128)S(1)} %collective-permute-done.2, f32[]{:T(128)} %bitcast.44, f32[]{:T(128)} %bitcast.43, f32[]{:T(128)} %bitcast.42, f32[]{:T(128)} %bitcast.41, ...), kind=kLoop, calls=%fused_computation.134 | loop fusion | flops 12189696 | bytes 1241172 | tf_op jit(solution)/shard_map/convert_element_type | solution.py:49
  76.0 0.2 copy.19
  76.2 0.2 copy.26
  76.4 0.0 copy-done.1
  76.4 0.0 copy-start.4
  76.4 1.8 convolution_bitcast_fusion.1
  78.2 114.9 %psum.7 = f32[256,24]{1,0:T(8,128)S(1)} all-reduce(f32[256,24]{1,0:T(8,128)S(1)} %convolution_bitcast_fusion.1), channel_id=1, replica_groups=mesh['gx'=32,'gy'=16] {'gx','gy'}, use_global_device_ids=true, to_apply=%region_0.0 | all-reduce | flops 6144 | bytes 49152 | tf_op jit(solution)/shard_map/psum | solution.py:56
  193.1 0.0 copy-done.4
  193.1 0.6 dynamic-slice_add_fusion
Async XLA Ops:
  0.0 3.1 %copy-start = (f32[6,6]{1,0:T(8,128)S(1)}, f32[6,6]{1,0:T(8,128)}, u32[]{:S(2)}) copy-start(f32[6,6]{1,0:T(8,128)} %param.9) | copy-start | bytes 436
  3.1 6.8 %copy-start.2 = (f32[21]{0:T(128)S(1)}, f32[21]{0:T(128)}, u32[]{:S(2)}) copy-start(f32[21]{0:T(128)} %param.10) | copy-start | bytes 256
  3.1 8.2 %copy-start.3 = (f32[21]{0:T(128)S(1)}, f32[21]{0:T(128)}, u32[]{:S(2)}) copy-start(f32[21]{0:T(128)} %param.11) | copy-start | bytes 256
  4.6 7.9 %collective-permute-start = (f32[4,6,10,256]{3,1,0,2:T(8,128)S(1)}, f32[4,6,10,256]{3,1,0,2:T(8,128)S(1)}, u32[]{:S(2)}, u32[]{:S(2)}) collective-permute-start(f32[4,6,10,256]{3,1,0,2:T(8,128)S(1)} %get-tuple-element.7), channel_id=1, source_target_pairs={{0,16},{16,32},{32,48},{48,64},{64,80},{80,96},{96,112},{112,128},... | collective-permute-start | bytes 737288 | tf_op jit(solution)/shard_map/ppermute | solution.py:12
  8.6 8.0 %collective-permute-start.1 = (f32[4,6,10,256]{3,1,0,2:T(8,128)S(1)}, f32[4,6,10,256]{3,1,0,2:T(8,128)S(1)}, u32[]{:S(2)}, u32[]{:S(2)}) collective-permute-start(f32[4,6,10,256]{3,1,0,2:T(8,128)S(1)} %get-tuple-element.8), channel_id=1, source_target_pairs={{16,0},{32,16},{48,32},{64,48},{80,64},{96,80},{112,96},{128,112},... | collective-permute-start | bytes 737288 | tf_op jit(solution)/shard_map/ppermute | solution.py:15
  32.6 16.2 %collective-permute-start.2 = (f32[4,6,32,10]{3,1,0,2:T(8,128)S(1)}, f32[4,6,32,10]{3,1,0,2:T(8,128)S(1)}, u32[]{:S(2)}, u32[]{:S(2)}) collective-permute-start(f32[4,6,32,10]{3,1,0,2:T(8,128)S(1)} %get-tuple-element.5), channel_id=1, source_target_pairs={{0,1},{1,2},{2,3},{3,4},{4,5},{5,6},{6,7},{7,8},{8,9},{9,10},{10,1... | collective-permute-start | bytes 92168 | tf_op jit(solution)/shard_map/ppermute | solution.py:12
  42.6 10.5 %collective-permute-start.3 = (f32[4,6,32,10]{3,1,0,2:T(8,128)S(1)}, f32[4,6,32,10]{3,1,0,2:T(8,128)S(1)}, u32[]{:S(2)}, u32[]{:S(2)}) collective-permute-start(f32[4,6,32,10]{3,1,0,2:T(8,128)S(1)} %get-tuple-element.6), channel_id=1, source_target_pairs={{1,0},{2,1},{3,2},{4,3},{5,4},{6,5},{7,6},{8,7},{9,8},{10,9},{11,1... | collective-permute-start | bytes 92168 | tf_op jit(solution)/shard_map/ppermute | solution.py:15
  53.1 23.3 %copy-start.1 = (bf16[32,256,256]{2,1,0:T(8,128)(2,1)S(1)}, bf16[32,256,256]{2,1,0:T(8,128)(2,1)}, u32[]{:S(2)}) copy-start(bf16[32,256,256]{2,1,0:T(8,128)(2,1)} %param.12) | copy-start | bytes 12582916
  76.4 116.7 %copy-start.4 = (f32[16,24]{1,0:T(8,128)S(1)}, f32[16,24]{1,0:T(8,128)}, u32[]{:S(2)}) copy-start(f32[16,24]{1,0:T(8,128)} %param.13) | copy-start | bytes 4612
where the time goes:
time: 194 us
  blocking collectives  115 us (59%)
  other arithmetic  39.2 us (20%)
  starting transfers between devices  17.2 us (9%)
  waiting for transfers between devices  12.4 us (6%)
  matrix products  6.28 us (3%)
  local copies, waits for them, and re-layouts  3.52 us (2%)
    psum x1, blocking collectives, local(): total = lax.psum(projection, ('gx', 'gy'))  115 us
    convert_element_type x1, other arithmetic, local(): smoothed = smoothed.astype(jnp.bfloat16)  22.8 us
    add x1, other arithmetic, smooth_valid(): total + taps[j] * lax.slice_in_dim(extended, j, j + count, axis=axis)  15.8 us
    ppermute x2, starting transfers between devices, padded(): lax.ppermute(lax.slice_in_dim(block, block.shape[dim] - width, None, axis...  14 us
    ppermute x2, waiting for transfers between devices, padded(): lax.ppermute(lax.slice_in_dim(block, 0, width, axis=dim), axis, backward)  8.37 us
    dot_general x2, matrix products, local(): jnp.einsum('gf,st,gsxy->ftxy', field_mixing, time_mixing, adjoint_forcing...  4.51 us
    ppermute x2, waiting for transfers between devices, padded(): lax.ppermute(lax.slice_in_dim(block, block.shape[dim] - width, None, axis...  4.06 us
  transfers between devices with their start and end apart: 4, of which 4 were waited for; matrix products, arithmetic and copies ran while one was open for 1% of the time, Pallas kernels for 0%

commit v1 on v0

--- a/solution.py
+++ b/solution.py
@@ -53,7 +53,8 @@
         flat_modes, flat_state, (((0,), (1,)), ((), ())), preferred_element_type=jnp.float32
     )
     owned = coefficients.shape[0]
-    total = lax.psum(projection, ("gx", "gy"))
+    inner = lax.psum(projection, "gy")
+    total = lax.psum(inner, "gx")
     mine = lax.dynamic_slice_in_dim(total, lax.axis_index("gy") * owned, owned, 0)
     return coefficients + mine
 

time: 194 us -> 280 us (1.44)
  the two profiles are of different devices: /device:TPU:1 before, /device:TPU:4 now
where the time goes in v1:
time: 280 us
  blocking collectives  200 us (71%)
  other arithmetic  39.3 us (14%)
  waiting for transfers between devices  16.5 us (6%)
  starting transfers between devices  13.6 us (5%)
  matrix products  6.27 us (2%)
  local copies, waits for them, and re-layouts  3.52 us (1%)
    psum x1, blocking collectives, local(): total = lax.psum(inner, 'gx')  129 us
    psum x1, blocking collectives, local(): inner = lax.psum(projection, 'gy')  71.2 us
    convert_element_type x1, other arithmetic, local(): smoothed = smoothed.astype(jnp.bfloat16)  22.7 us
    add x1, other arithmetic, smooth_valid(): total + taps[j] * lax.slice_in_dim(extended, j, j + count, axis=axis)  15.9 us
    ppermute x2, waiting for transfers between devices, padded(): lax.ppermute(lax.slice_in_dim(block, block.shape[dim] - width, None, axis...  14.8 us
    ppermute x2, starting transfers between devices, padded(): lax.ppermute(lax.slice_in_dim(block, 0, width, axis=dim), axis, backward)  8.55 us
  transfers between devices with their start and end apart: 4, of which 3 were waited for; matrix products, arithmetic and copies ran while one was open for 1% of the time, Pallas kernels for 0%

profile of v1, /device:TPU:4, one launch (start us, length us, event | category | flops | bytes accessed | tf_op | source)
XLA Modules:
  0.0 279.6 jit_solution(9277061477830819370)
XLA Ops:
  0.0 0.0 copy-start
  0.0 3.1 %fusion.118 = f32[6,32,256,4]{2,3,1,0:T(4,128)S(1)} fusion(f32[4,6,32,256]{3,2,1,0:T(8,128)} %param.7, f32[4,4]{1,0:T(4,128)} %param.8), kind=kOutput, calls=%fused_computation.196 | convolution fusion | flops 9437184 | bytes 1572928 | tf_op jit(solution)/shard_map/gf,st,gsxy->ftxy/dot_general | solution.py:38
  3.1 0.0 copy-done
  3.1 0.0 copy-start.2
  3.1 0.0 copy-start.3
  3.1 1.5 convolution_bitcast_fusion
  4.6 0.1 fusion.123
  4.6 3.1 %collective-permute-start = (f32[4,6,10,256]{3,1,0,2:T(8,128)S(1)}, f32[4,6,10,256]{3,1,0,2:T(8,128)S(1)}, u32[]{:S(2)}, u32[]{:S(2)}) collective-permute-start(f32[4,6,10,256]{3,1,0,2:T(8,128)S(1)} %get-tuple-element.7), channel_id=1, source_target_pairs={{0,16},{16,32},{32,48},{48,64},{64,80},{80,96},{96,112},{112,128},... | collective-permute-start | bytes 737288 | tf_op jit(solution)/shard_map/ppermute | solution.py:12
  7.7 1.3 collective-permute-start.1
  9.0 0.0 copy-done.2
  9.1 0.7 fusion.127
  9.7 0.7 fusion.126
  10.4 0.0 copy-done.3
  10.5 0.7 fusion.124
  11.2 10.5 %collective-permute-done = f32[4,6,10,256]{3,1,0,2:T(8,128)S(1)} collective-permute-done((f32[4,6,10,256]{3,1,0,2:T(8,128)S(1)}, f32[4,6,10,256]{3,1,0,2:T(8,128)S(1)}, u32[]{:S(2)}, u32[]{:S(2)}) %collective-permute-start) | collective-permute-done | bytes 245792 | tf_op jit(solution)/shard_map/ppermute | solution.py:12
  21.7 0.0 collective-permute-done.1
  21.7 15.9 %fusion.3 = f32[4,6,32,256]{3,1,0,2:T(8,128)S(1)} fusion(f32[4,6,32,256]{3,1,0,2:T(8,128)S(1)} %convolution_bitcast_fusion, f32[4,6,10,256]{3,1,0,2:T(8,128)S(1)} %collective-permute-done.1, f32[4,6,10,256]{3,1,0,2:T(8,128)S(1)} %collective-permute-done, f32[]{:T(128)} %bitcast.24, f32[]{:T(128)} %bitcast.23, f32[]{:T(128)} %bitcast.22, f32[]{:T(128)} %bitcast.21, ...), kind=kLoop, calls=%fused_computation.77 | loop fusion | flops 11993088 | bytes 2064468 | tf_op jit(solution)/shard_map/add | solution.py:23
  37.7 0.2 fusion.122
  37.9 1.9 collective-permute-start.2
  39.8 7.3 %collective-permute-start.3 = (f32[4,6,32,10]{3,1,0,2:T(8,128)S(1)}, f32[4,6,32,10]{3,1,0,2:T(8,128)S(1)}, u32[]{:S(2)}, u32[]{:S(2)}) collective-permute-start(f32[4,6,32,10]{3,1,0,2:T(8,128)S(1)} %get-tuple-element.6), channel_id=1, source_target_pairs={{1,0},{2,1},{3,2},{4,3},{5,4},{6,5},{7,6},{8,7},{9,8},{10,9},{11,1... | collective-permute-start | bytes 92168 | tf_op jit(solution)/shard_map/ppermute | solution.py:15
  47.1 0.7 fusion.125
  47.7 4.3 %collective-permute-done.2 = f32[4,6,32,10]{3,1,0,2:T(8,128)S(1)} collective-permute-done((f32[4,6,32,10]{3,1,0,2:T(8,128)S(1)}, f32[4,6,32,10]{3,1,0,2:T(8,128)S(1)}, u32[]{:S(2)}, u32[]{:S(2)}) %collective-permute-start.2) | collective-permute-done | bytes 30752 | tf_op jit(solution)/shard_map/ppermute | solution.py:12
  52.0 1.8 collective-permute-done.3
  53.7 0.0 copy-start.1
  53.7 22.7 %fusion.60 = bf16[4,6,32,256]{3,1,0,2:T(8,128)(2,1)S(1)} fusion(f32[4,6,32,256]{3,1,0,2:T(8,128)S(1)} %fusion.3, f32[4,6,32,10]{3,1,0,2:T(8,128)S(1)} %collective-permute-done.3, f32[4,6,32,10]{3,1,0,2:T(8,128)S(1)} %collective-permute-done.2, f32[]{:T(128)} %bitcast.44, f32[]{:T(128)} %bitcast.43, f32[]{:T(128)} %bitcast.42, f32[]{:T(128)} %bitcast.41, ...), kind=kLoop, calls=%fused_computation.134 | loop fusion | flops 12189696 | bytes 1241172 | tf_op jit(solution)/shard_map/convert_element_type | solution.py:49
  76.5 0.2 copy.19
  76.7 0.2 copy.26
  77.0 0.0 copy-done.1
  77.0 0.0 copy-start.4
  77.0 1.8 convolution_bitcast_fusion.1
  78.8 71.2 %psum.14 = f32[256,24]{1,0:T(8,128)S(1)} all-reduce(f32[256,24]{1,0:T(8,128)S(1)} %convolution_bitcast_fusion.1), channel_id=1, replica_groups=mesh['gx'=32,'gy'=16] {'gy'}, use_global_device_ids=true, to_apply=%region_0.0 | all-reduce | flops 6144 | bytes 49152 | tf_op jit(solution)/shard_map/psum | solution.py:56
  149.9 129.0 %psum.15 = f32[256,24]{1,0:T(8,128)S(1)} all-reduce(f32[256,24]{1,0:T(8,128)S(1)} %psum.14), channel_id=1, replica_groups=mesh['gx'=32,'gy'=16] {'gx'}, use_global_device_ids=true, to_apply=%region_1.0 | all-reduce | flops 6144 | bytes 49152 | tf_op jit(solution)/shard_map/psum | solution.py:57
  279.0 0.0 copy-done.4
  279.0 0.6 dynamic-slice_add_fusion
Async XLA Ops:
  0.0 3.1 %copy-start = (f32[6,6]{1,0:T(8,128)S(1)}, f32[6,6]{1,0:T(8,128)}, u32[]{:S(2)}) copy-start(f32[6,6]{1,0:T(8,128)} %param.9) | copy-start | bytes 436
  3.1 6.0 %copy-start.2 = (f32[21]{0:T(128)S(1)}, f32[21]{0:T(128)}, u32[]{:S(2)}) copy-start(f32[21]{0:T(128)} %param.10) | copy-start | bytes 256
  3.1 7.4 %copy-start.3 = (f32[21]{0:T(128)S(1)}, f32[21]{0:T(128)}, u32[]{:S(2)}) copy-start(f32[21]{0:T(128)} %param.11) | copy-start | bytes 256
  4.6 17.1 %collective-permute-start = (f32[4,6,10,256]{3,1,0,2:T(8,128)S(1)}, f32[4,6,10,256]{3,1,0,2:T(8,128)S(1)}, u32[]{:S(2)}, u32[]{:S(2)}) collective-permute-start(f32[4,6,10,256]{3,1,0,2:T(8,128)S(1)} %get-tuple-element.7), channel_id=1, source_target_pairs={{0,16},{16,32},{32,48},{48,64},{64,80},{80,96},{96,112},{112,128},... | collective-permute-start | bytes 737288 | tf_op jit(solution)/shard_map/ppermute | solution.py:12
  7.7 14.0 %collective-permute-start.1 = (f32[4,6,10,256]{3,1,0,2:T(8,128)S(1)}, f32[4,6,10,256]{3,1,0,2:T(8,128)S(1)}, u32[]{:S(2)}, u32[]{:S(2)}) collective-permute-start(f32[4,6,10,256]{3,1,0,2:T(8,128)S(1)} %get-tuple-element.8), channel_id=1, source_target_pairs={{16,0},{32,16},{48,32},{64,48},{80,64},{96,80},{112,96},{128,112},... | collective-permute-start | bytes 737288 | tf_op jit(solution)/shard_map/ppermute | solution.py:15
  37.9 14.1 %collective-permute-start.2 = (f32[4,6,32,10]{3,1,0,2:T(8,128)S(1)}, f32[4,6,32,10]{3,1,0,2:T(8,128)S(1)}, u32[]{:S(2)}, u32[]{:S(2)}) collective-permute-start(f32[4,6,32,10]{3,1,0,2:T(8,128)S(1)} %get-tuple-element.5), channel_id=1, source_target_pairs={{0,1},{1,2},{2,3},{3,4},{4,5},{5,6},{6,7},{7,8},{8,9},{9,10},{10,1... | collective-permute-start | bytes 92168 | tf_op jit(solution)/shard_map/ppermute | solution.py:12
  39.8 13.9 %collective-permute-start.3 = (f32[4,6,32,10]{3,1,0,2:T(8,128)S(1)}, f32[4,6,32,10]{3,1,0,2:T(8,128)S(1)}, u32[]{:S(2)}, u32[]{:S(2)}) collective-permute-start(f32[4,6,32,10]{3,1,0,2:T(8,128)S(1)} %get-tuple-element.6), channel_id=1, source_target_pairs={{1,0},{2,1},{3,2},{4,3},{5,4},{6,5},{7,6},{8,7},{9,8},{10,9},{11,1... | collective-permute-start | bytes 92168 | tf_op jit(solution)/shard_map/ppermute | solution.py:15
  53.7 23.2 %copy-start.1 = (bf16[32,256,256]{2,1,0:T(8,128)(2,1)S(1)}, bf16[32,256,256]{2,1,0:T(8,128)(2,1)}, u32[]{:S(2)}) copy-start(bf16[32,256,256]{2,1,0:T(8,128)(2,1)} %param.12) | copy-start | bytes 12582916
  77.0 202.0 %copy-start.4 = (f32[16,24]{1,0:T(8,128)S(1)}, f32[16,24]{1,0:T(8,128)}, u32[]{:S(2)}) copy-start(f32[16,24]{1,0:T(8,128)} %param.13) | copy-start | bytes 4612
